TPU v7x, 256 devices: a whole 4x4x8 slice. The times are simulated.
256 devices in a mesh: wide: 32 (over y, x, core), narrow: 8 (over z).
Axes of the slice: x: 4, y: 4, z: 8, core: 2. Of those that a mesh axis runs over, the one named last changes fastest.
Arguments:
- three_centre: bfloat16 [32, 1024, 4096], P('narrow', 'wide'), may hold values from -6 to 6
- go_blocks: bfloat16 [64, 64, 64], replicated, may hold values from -0.75 to 0.75
- gv_blocks: bfloat16 [64, 64, 64], replicated, may hold values from -0.125 to 0.125
- go_index: int32 [32, 32], P('narrow'), may hold values from 0 to 63
- gv_index: int32 [32, 32], P('narrow'), may hold values from 0 to 63
- source_mask: int32 [32, 32], P('narrow'), may hold values 0 or 1
Outputs:
- chi: float32 [1024, 1024], P('wide', 'narrow')
All inputs are finite; a program needn't handle non-finite values. No bound on the sum of `source_mask` on one device may be relied on, other than what follows from the above.
Results may differ from a plain program's by a relative error of at most 0.004.
Values may be sent and summed in bfloat16 or wider, within the bound.
No kernel may reach another device: no remote copies, remote signals or barrier semaphores. Data moves between devices by JAX's collectives and lax.ppermute only.
A program may use at most 192 MiB of HBM per device.

v0:
```python
import jax
import jax.numpy as jnp
from jax import lax
from jax.sharding import PartitionSpec as P


def local(three_centre, go_blocks, gv_blocks, go_index, gv_index, source_mask):
    local_pairs, aux_local, pair_width = three_centre.shape
    block = go_blocks.shape[1]
    go_chosen = go_blocks[go_index]
    gv_chosen = gv_blocks[gv_index] * source_mask.astype(jnp.bfloat16)[:, :, None, None]
    piece = lax.all_gather(three_centre, "narrow", axis=0, tiled=True)
    number_sources = piece.shape[0]
    sources = piece.reshape(number_sources, aux_local, block, block)
    results = []
    for target in range(local_pairs):
        first_product = jnp.einsum(
            "cma,cpmn->cpan", go_chosen[target], sources, preferred_element_type=jnp.float32
        ).astype(jnp.bfloat16)
        results.append(
            jnp.einsum(
                "cpan,cnd->pad",
                first_product,
                gv_chosen[target],
                preferred_element_type=jnp.float32,
            )
        )
    summed = jnp.stack(results)
    image = summed.reshape(local_pairs, aux_local, pair_width).astype(jnp.bfloat16)
    norm_scale = 1.0 / jnp.sqrt(jnp.float32(local_pairs * lax.axis_size("narrow") * pair_width))
    partial_chi = jnp.einsum(
        "kpe,kqe->pq",
        image,
        lax.all_gather(three_centre, "wide", axis=1, tiled=True),
        preferred_element_type=jnp.float32,
    )
    result = lax.psum_scatter(partial_chi, "narrow", scatter_dimension=1, tiled=True)
    return result * norm_scale


def solution(mesh):
    placed = (
        P("narrow", "wide", None),
        P(),
        P(),
        P("narrow", None),
        P("narrow", None),
        P("narrow", None),
    )
    return jax.shard_map(
        local, mesh=mesh, in_specs=placed, out_specs=P("wide", "narrow"), check_vma=False
    )
```

profile of v0, /device:TPU:12, one launch (start us, length us, event | category | flops | bytes accessed | tf_op | source)
XLA Modules:
  0.0 286.2 jit_solution(9310431331818708807)
XLA Ops:
  6.5 0.7 all-gather.3.cloned.1.call-update
  7.3 0.7 all-gather.5.cloned.1.call-update
  8.1 0.7 compare_select_fusion
  8.7 0.1 reshape.28
  8.8 0.7 convert_element_type.30
  9.5 0.7 compare_select_fusion.1
  10.2 0.1 reshape.20
  10.3 1.0 gather_fusion.1
  11.3 3.4 %gather_fusion = bf16[128,64,64]{2,1,0:T(8,128)(2,1)} fusion(bf16[64,64,64]{2,1,0:T(8,128)(2,1)} %param.7, s32[1024]{0:T(1024)S(1)} %pad_clamp_fusion.1), kind=kCustom, calls=%fused_computation | custom fusion | bytes 2097664 | tf_op jit(solution)/shard_map/gather | solution.py:10
  14.7 1.5 broadcast_multiply_fusion
  16.2 90.0 %all-gather.3.cloned.1.call-done = bf16[32,32,4096]{2,1,0:T(8,128)(2,1)} async-done(((bf16[4,32,4096]{2,1,0:T(8,128)(2,1)}), bf16[32,32,4096]{2,1,0:T(8,128)(2,1)}) %all-gather.3.cloned.1.call-update) | async-done | bytes 8388624 | tf_op jit(solution)/shard_map/all_gather | solution.py:12
  106.2 23.6 %reshape.17 = bf16[32,32,64,64]{3,2,1,0:T(8,128)(2,1)} reshape(bf16[32,32,4096]{2,1,0:T(8,128)(2,1)} %all-gather.3.cloned.1.call-done) | data formatting | bytes 16777216 | tf_op jit(solution)/shard_map/reshape | solution.py:14
  129.8 10.7 %fusion.63 = bf16[32,64,64]{2,1,0:T(8,128)(2,1)S(1)} fusion(bf16[32,32,64,64]{3,2,1,0:T(8,128)(2,1)} %reshape.17, bf16[4,32,64,64]{3,2,1,0:T(8,128)(2,1)S(1)} %copy-done.2, bf16[128,64,64]{2,1,0:T(8,128)(2,1)} %gather_fusion), kind=kOutput, calls=%fused_computation.29 | convolution fusion | flops 1078067200 | bytes 18087936 | tf_op jit(solution)/shard_map/cpan,cnd->pad/dot_general | solution.py:21
  140.6 0.5 stack.15
  141.0 10.6 %fusion.58 = bf16[32,64,64]{2,1,0:T(8,128)(2,1)S(1)} fusion(bf16[32,32,64,64]{3,2,1,0:T(8,128)(2,1)} %reshape.17, bf16[4,32,64,64]{3,2,1,0:T(8,128)(2,1)S(1)} %copy-done.2, bf16[128,64,64]{2,1,0:T(8,128)(2,1)} %gather_fusion), kind=kOutput, calls=%fused_computation.28 | convolution fusion | flops 1078067200 | bytes 18087936 | tf_op jit(solution)/shard_map/cpan,cnd->pad/dot_general | solution.py:21
  151.6 1.2 stack.16
  152.8 12.7 %fusion.53 = bf16[32,64,64]{2,1,0:T(8,128)(2,1)S(1)} fusion(bf16[32,32,64,64]{3,2,1,0:T(8,128)(2,1)} %reshape.17, bf16[4,32,64,64]{3,2,1,0:T(8,128)(2,1)S(1)} %copy-done.2, bf16[128,64,64]{2,1,0:T(8,128)(2,1)} %gather_fusion), kind=kOutput, calls=%fused_computation.27 | convolution fusion | flops 1078067200 | bytes 18087936 | tf_op jit(solution)/shard_map/cpan,cnd->pad/dot_general | solution.py:21
  165.5 1.2 stack.17
  166.7 11.7 %fusion.48 = bf16[32,64,64]{2,1,0:T(8,128)(2,1)} fusion(bf16[32,32,64,64]{3,2,1,0:T(8,128)(2,1)} %reshape.17, bf16[4,32,64,64]{3,2,1,0:T(8,128)(2,1)S(1)} %copy-done.2, bf16[128,64,64]{2,1,0:T(8,128)(2,1)} %gather_fusion), kind=kOutput, calls=%fused_computation.26 | convolution fusion | flops 1078067200 | bytes 18087936 | tf_op jit(solution)/shard_map/cpan,cnd->pad/dot_general | solution.py:21
  178.4 1.6 stack.18
  180.0 44.6 %all-gather.5.cloned.1.call-done = bf16[4,1024,4096]{2,1,0:T(8,128)(2,1)} async-done(((bf16[4,32,4096]{2,1,0:T(8,128)(2,1)}), bf16[4,1024,4096]{2,1,0:T(8,128)(2,1)}) %all-gather.5.cloned.1.call-update) | async-done | bytes 33554448 | tf_op jit(solution)/shard_map/all_gather | solution.py:34
  224.6 16.0 %convolution_bitcast_fusion = f32[32,1024]{1,0:T(8,128)} fusion(bf16[4,1024,4096]{2,1,0:T(8,128)(2,1)} %all-gather.5.cloned.1.call-done, bf16[1,32,4096]{2,1,0:T(8,128)(2,1)S(1)} %stack.18, bf16[1,32,4096]{2,1,0:T(8,128)(2,1)} %stack.17, bf16[1,32,4096]{2,1,0:T(8,128)(2,1)} %stack.16, bf16[1,32,4096]{2,1,0:T(8,128)(2,1)S(1)} %stack.15), kind=kOutput, calls=%fused_computation.30 | convolution fusion | flops 1075314688 | bytes 34734080 | tf_op jit(solution)/shard_map/kpe,kqe->pq/dot_general | solution.py:31
  240.6 37.7 %reduce-scatter.2.cloned.1.call-done = f32[32,128]{1,0:T(8,128)} async-done(((f32[32,1024]{1,0:T(8,128)}), f32[32,128]{1,0:T(8,128)}) %reduce-scatter.2.cloned.1.call-update) | async-done | bytes 16400 | tf_op jit(solution)/shard_map/reduce_scatter | solution.py:37
  278.4 1.3 broadcast_multiply_fusion.1
  (12 shorter events, 0.1 us)
Async XLA Ops:
  6.5 3.8 %copy-start = (bf16[64,64,64]{2,1,0:T(8,128)(2,1)S(1)}, bf16[64,64,64]{2,1,0:T(8,128)(2,1)}, u32[]{:S(2)}) copy-start(bf16[64,64,64]{2,1,0:T(8,128)(2,1)} %param.8) | copy-start | bytes 1572868
  6.5 99.6 %all-gather.3.cloned.1.call-start = ((), (), s32[]{:S(2)}) async-start(), calls=%async_computation.1 | async-start | bytes 9437184 | tf_op jit(solution)/shard_map/all_gather | solution.py:12
  7.3 217.3 %all-gather.5.cloned.1.call-start = ((), (), s32[]{:S(2)}) async-start(), calls=%async_computation.2 | async-start | bytes 34603008 | tf_op jit(solution)/shard_map/all_gather | solution.py:34
  8.0 270.4 %reduce-scatter.2.cloned.1.call-start = ((), (), s32[]{:S(2)}) async-start(), calls=%async_computation.3 | async-start | bytes 147456 | tf_op jit(solution)/shard_map/reduce_scatter | solution.py:37
  16.2 113.6 %copy-start.2 = (bf16[4,32,64,64]{3,2,1,0:T(8,128)(2,1)S(1)}, bf16[4,32,64,64]{3,2,1,0:T(8,128)(2,1)}, u32[]{:S(2)}) copy-start(bf16[4,32,64,64]{3,2,1,0:T(8,128)(2,1)} %broadcast_multiply_fusion) | copy-start | bytes 3145732
  178.4 101.3 %copy-start.1 = (bf16[64,64,64]{2,1,0:T(8,128)(2,1)S(1)}, bf16[64,64,64]{2,1,0:T(8,128)(2,1)}, u32[]{:S(2)}) copy-start(bf16[64,64,64]{2,1,0:T(8,128)(2,1)} %param.8) | copy-start | bytes 1572868
Sparse Core Ops, SparseCore 0:
  9.1 96.9 all-gather.2
  108.8 115.7 all-gather.4
  240.7 37.5 reduce-scatter.1
where the time goes:
time: 287 us; the launch traced here: 286 us
  waiting for transfers between devices  174 us (61%)
  matrix products  61.8 us (22%)
  local copies, waits for them, and re-layouts  32.6 us (11%)
  between operations  13.2 us (5%)
  other arithmetic  4.92 us (2%)
    all_gather x1, waiting for transfers between devices, local(): piece = lax.all_gather(three_centre, 'narrow', axis=0, tiled=True)  90 us
    dot_general x4, matrix products, local(): jnp.einsum('cpan,cnd->pad', first_product, gv_chosen[target], preferred_e...  45.7 us
    all_gather x1, waiting for transfers between devices, local(): lax.all_gather(three_centre, 'wide', axis=1, tiled=True)  44.6 us
    reduce_scatter x1, waiting for transfers between devices, local(): lax.psum_scatter(partial_chi, 'narrow', scatter_dimension=1, tiled=True)  37.7 us
    reshape x1, local copies, waits for them, and re-layouts, local(): sources = piece.reshape(number_sources, aux_local, block, block)  23.6 us
    dot_general x1, matrix products, local(): jnp.einsum('kpe,kqe->pq', image, lax.all_gather(three_centre, 'wide', axi...  16 us
  transfers between devices with their start and end apart: 3, of which 3 were waited for; matrix products, arithmetic and copies ran while one was open for 29% of the time, Pallas kernels for 0%

commit v1 on v0

--- a/solution.py
+++ b/solution.py
@@ -2,6 +2,13 @@
 import jax.numpy as jnp
 from jax import lax
 from jax.sharding import PartitionSpec as P
+
+
+def exchange_gather(shard, mesh_axis, along):
+    size = lax.axis_size(mesh_axis)
+    blocks = jnp.stack([shard for _ in range(size)])
+    blocks = lax.all_to_all(blocks, mesh_axis, split_axis=0, concat_axis=0)
+    return jnp.concatenate(blocks, axis=along)
 
 
 def local(three_centre, go_blocks, gv_blocks, go_index, gv_index, source_mask):
@@ -9,7 +16,7 @@
     block = go_blocks.shape[1]
     go_chosen = go_blocks[go_index]
     gv_chosen = gv_blocks[gv_index] * source_mask.astype(jnp.bfloat16)[:, :, None, None]
-    piece = lax.all_gather(three_centre, "narrow", axis=0, tiled=True)
+    piece = exchange_gather(three_centre, "narrow", 0)
     number_sources = piece.shape[0]
     sources = piece.reshape(number_sources, aux_local, block, block)
     results = []

time: 287 us -> 337 us (1.17)
  waiting for transfers between devices: 174 us -> 214 us
  starting transfers between devices: 0.08 us -> 8.54 us
  local copies, waits for them, and re-layouts: 32.6 us -> 38 us
    all_to_all x0 -> x1, waiting for transfers between devices: none -> 180 us  [exchange_gather(): blocks = lax.all_to_all(blocks, mesh_axis, split_axis=0, concat_axis=0)]
    all_gather x1 -> x0, waiting for transfers between devices: 90 us -> none  [local(): piece = lax.all_gather(three_centre, 'narrow', axis=0, tiled=True)]
    all_gather x1, waiting for transfers between devices: 44.6 us -> 0.02 us  [local(): lax.all_gather(three_centre, 'wide', axis=1, tiled=True)]
    another operation x0 -> x2, local copies, waits for them, and re-layouts: none -> 29.1 us  [the longest x1 23.6 us: local(): sources = piece.reshape(number_sources, aux_local, block, block)]
    reshape x1 -> x0, local copies, waits for them, and re-layouts: 23.6 us -> none  [local(): sources = piece.reshape(number_sources, aux_local, block, block)]
    all_to_all x0 -> x1, starting transfers between devices: none -> 8.47 us  [exchange_gather(): blocks = lax.all_to_all(blocks, mesh_axis, split_axis=0, concat_axis=0)]
    reduce_scatter x1, waiting for transfers between devices: 37.7 us -> 32.9 us  [local(): lax.psum_scatter(partial_chi, 'narrow', scatter_dimension=1, tiled=True)]
  transfers between devices with their start and end apart: 3 -> 3, of which waited for: 3 -> 2; matrix products, arithmetic and copies ran while one was open for 29% -> 25% of each run, Pallas kernels for 0% -> 0%
where the time goes in v1:
time: 337 us; the launch traced here: 336 us
  waiting for transfers between devices  214 us (64%)
  matrix products  59 us (18%)
  local copies, waits for them, and re-layouts  38 us (11%)
  between operations  13.5 us (4%)
  starting transfers between devices  8.54 us (3%)
    all_to_all x1, waiting for transfers between devices, exchange_gather(): blocks = lax.all_to_all(blocks, mesh_axis, split_axis=0, concat_axis=0)  180 us
    dot_general x4, matrix products, local(): jnp.einsum('cpan,cnd->pad', first_product, gv_chosen[target], preferred_e...  43 us
    reduce_scatter x1, waiting for transfers between devices, local(): lax.psum_scatter(partial_chi, 'narrow', scatter_dimension=1, tiled=True)  32.9 us
    another operation x1, local copies, waits for them, and re-layouts, local(): sources = piece.reshape(number_sources, aux_local, block, block)  23.6 us
    dot_general x1, matrix products, local(): jnp.einsum('kpe,kqe->pq', image, lax.all_gather(three_centre, 'wide', axi...  16 us
    all_to_all x1, starting transfers between devices, exchange_gather(): blocks = lax.all_to_all(blocks, mesh_axis, split_axis=0, concat_axis=0)  8.47 us
  transfers between devices with their start and end apart: 3, of which 2 were waited for; matrix products, arithmetic and copies ran while one was open for 25% of the time, Pallas kernels for 0%

profile of v1, /device:TPU:12, one launch (start us, length us, event | category | flops | bytes accessed | tf_op | source)
XLA Modules:
  0.0 336.0 jit_solution(11022660631016363681)
XLA Ops:
  6.5 0.0 all-gather.2.cloned.1.call-start
  6.6 0.7 all-gather.2.cloned.1.call-update
  7.3 5.5 %stack.12 = bf16[8,4,32,4096]{3,2,1,0:T(8,128)(2,1)} broadcast(bf16[4,32,4096]{2,1,0:T(8,128)(2,1)} %param.6), dimensions={1,2,3} | broadcast | bytes 9437184 | tf_op jit(solution)/shard_map/stack | solution.py:9
  12.8 8.5 %all-to-all-start = ((bf16[8,4,32,4096]{3,2,1,0:T(8,128)(2,1)}), bf16[8,4,32,4096]{3,2,1,0:T(8,128)(2,1)}, u32[]{:S(2)}, u32[]{:S(2)}) async-start(bf16[8,4,32,4096]{3,2,1,0:T(8,128)(2,1)} %stack.12), calls=%async_computation | async-start | bytes 16777216 | tf_op jit(solution)/shard_map/all_to_all | solution.py:10
  21.2 0.0 reduce-scatter.2.cloned.1.call-start
  21.3 0.1 reshape.26
  21.4 0.1 reshape.18
  21.5 1.0 gather_fusion.1
  22.5 3.4 %gather_fusion = bf16[128,64,64]{2,1,0:T(8,128)(2,1)} fusion(bf16[64,64,64]{2,1,0:T(8,128)(2,1)} %param.7, s32[1024]{0:T(1024)S(1)} %pad_clamp_fusion.1), kind=kCustom, calls=%fused_computation | custom fusion | bytes 2097664 | tf_op jit(solution)/shard_map/gather | solution.py:17
  25.9 1.5 broadcast_multiply_fusion
  27.4 180.4 %all-to-all-done = bf16[8,4,32,4096]{3,2,1,0:T(8,128)(2,1)} async-done(((bf16[8,4,32,4096]{3,2,1,0:T(8,128)(2,1)}), bf16[8,4,32,4096]{3,2,1,0:T(8,128)(2,1)}, u32[]{:S(2)}, u32[]{:S(2)}) %all-to-all-start) | async-done | bytes 8388640 | tf_op jit(solution)/shard_map/all_to_all | solution.py:10
  207.8 23.6 %reshape_reshape.3 = bf16[32,32,64,64]{3,2,1,0:T(8,128)(2,1)} reshape(bf16[8,4,32,4096]{3,2,1,0:T(8,128)(2,1)} %all-to-all-done) | data formatting | bytes 16777216 | tf_op jit(solution)/shard_map/reshape;reshape | solution.py:21
  231.4 10.6 %fusion.63 = bf16[32,64,64]{2,1,0:T(8,128)(2,1)S(1)} fusion(bf16[32,32,64,64]{3,2,1,0:T(8,128)(2,1)} %reshape_reshape.3, bf16[4,32,64,64]{3,2,1,0:T(8,128)(2,1)S(1)} %copy-done.2, bf16[128,64,64]{2,1,0:T(8,128)(2,1)} %gather_fusion), kind=kOutput, calls=%fused_computation.29 | convolution fusion | flops 1078067200 | bytes 18087936 | tf_op jit(solution)/shard_map/cpan,cnd->pad/dot_general | solution.py:28
  242.0 0.5 stack.13
  242.5 10.6 %fusion.58 = bf16[32,64,64]{2,1,0:T(8,128)(2,1)S(1)} fusion(bf16[32,32,64,64]{3,2,1,0:T(8,128)(2,1)} %reshape_reshape.3, bf16[4,32,64,64]{3,2,1,0:T(8,128)(2,1)S(1)} %copy-done.2, bf16[128,64,64]{2,1,0:T(8,128)(2,1)} %gather_fusion), kind=kOutput, calls=%fused_computation.28 | convolution fusion | flops 1078067200 | bytes 18087936 | tf_op jit(solution)/shard_map/cpan,cnd->pad/dot_general | solution.py:28
  253.1 1.2 stack.28
  254.2 10.6 %fusion.53 = bf16[32,64,64]{2,1,0:T(8,128)(2,1)S(1)} fusion(bf16[32,32,64,64]{3,2,1,0:T(8,128)(2,1)} %reshape_reshape.3, bf16[4,32,64,64]{3,2,1,0:T(8,128)(2,1)S(1)} %copy-done.2, bf16[128,64,64]{2,1,0:T(8,128)(2,1)} %gather_fusion), kind=kOutput, calls=%fused_computation.27 | convolution fusion | flops 1078067200 | bytes 18087936 | tf_op jit(solution)/shard_map/cpan,cnd->pad/dot_general | solution.py:28
  264.8 1.2 stack.29
  266.0 11.3 %fusion.48 = bf16[32,64,64]{2,1,0:T(8,128)(2,1)} fusion(bf16[32,32,64,64]{3,2,1,0:T(8,128)(2,1)} %reshape_reshape.3, bf16[4,32,64,64]{3,2,1,0:T(8,128)(2,1)S(1)} %copy-done.2, bf16[128,64,64]{2,1,0:T(8,128)(2,1)} %gather_fusion), kind=kOutput, calls=%fused_computation.26 | convolution fusion | flops 1078067200 | bytes 18087936 | tf_op jit(solution)/shard_map/cpan,cnd->pad/dot_general | solution.py:28
  277.3 1.6 stack.30
  278.9 0.0 all-gather.2.cloned.1.call-done
  278.9 16.0 %convolution_bitcast_fusion = f32[32,1024]{1,0:T(8,128)} fusion(bf16[4,1024,4096]{2,1,0:T(8,128)(2,1)} %all-gather.2.cloned.1.call-done, bf16[1,32,4096]{2,1,0:T(8,128)(2,1)S(1)} %stack.30, bf16[1,32,4096]{2,1,0:T(8,128)(2,1)} %stack.29, bf16[1,32,4096]{2,1,0:T(8,128)(2,1)} %stack.28, bf16[1,32,4096]{2,1,0:T(8,128)(2,1)S(1)} %stack.13), kind=kOutput, calls=%fused_computation.30 | convolution fusion | flops 1075314688 | bytes 34734080 | tf_op jit(solution)/shard_map/kpe,kqe->pq/dot_general | solution.py:38
  294.9 32.9 %reduce-scatter.2.cloned.1.call-done = f32[32,128]{1,0:T(8,128)} async-done(((f32[32,1024]{1,0:T(8,128)}), f32[32,128]{1,0:T(8,128)}) %reduce-scatter.2.cloned.1.call-update) | async-done | bytes 16400 | tf_op jit(solution)/shard_map/reduce_scatter | solution.py:44
  327.9 1.3 broadcast_multiply_fusion.1
  (18 shorter events, 0.1 us)
Async XLA Ops:
  6.5 15.0 %copy-start = (bf16[64,64,64]{2,1,0:T(8,128)(2,1)S(1)}, bf16[64,64,64]{2,1,0:T(8,128)(2,1)}, u32[]{:S(2)}) copy-start(bf16[64,64,64]{2,1,0:T(8,128)(2,1)} %param.8) | copy-start | bytes 1572868
  6.5 14.7 %copy-start.4 = (s32[4,32]{1,0:T(4,128)S(1)}, s32[4,32]{1,0:T(4,128)}, u32[]{:S(2)}) copy-start(s32[4,32]{1,0:T(4,128)} %param.10) | copy-start | bytes 1540
  6.5 14.8 %copy-start.3 = (s32[4,32]{1,0:T(4,128)S(1)}, s32[4,32]{1,0:T(4,128)}, u32[]{:S(2)}) copy-start(s32[4,32]{1,0:T(4,128)} %param.11) | copy-start | bytes 1540
  6.5 14.8 %copy-start.5 = (s32[4,32]{1,0:T(4,128)S(1)}, s32[4,32]{1,0:T(4,128)}, u32[]{:S(2)}) copy-start(s32[4,32]{1,0:T(4,128)} %param.9) | copy-start | bytes 1540
  6.5 272.3 %all-gather.2.cloned.1.call-start = ((), (), s32[]{:S(2)}) async-start(), calls=%async_computation.2 | async-start | bytes 34603008 | tf_op jit(solution)/shard_map/all_gather | solution.py:41
  12.8 195.1 %all-to-all-start = ((bf16[8,4,32,4096]{3,2,1,0:T(8,128)(2,1)}), bf16[8,4,32,4096]{3,2,1,0:T(8,128)(2,1)}, u32[]{:S(2)}, u32[]{:S(2)}) async-start(bf16[8,4,32,4096]{3,2,1,0:T(8,128)(2,1)} %stack.12), calls=%async_computation | async-start | bytes 16777216 | tf_op jit(solution)/shard_map/all_to_all | solution.py:10
  21.2 306.6 %reduce-scatter.2.cloned.1.call-start = ((), (), s32[]{:S(2)}) async-start(), calls=%async_computation.3 | async-start | bytes 147456 | tf_op jit(solution)/shard_map/reduce_scatter | solution.py:44
  27.4 204.0 %copy-start.2 = (bf16[4,32,64,64]{3,2,1,0:T(8,128)(2,1)S(1)}, bf16[4,32,64,64]{3,2,1,0:T(8,128)(2,1)}, u32[]{:S(2)}) copy-start(bf16[4,32,64,64]{3,2,1,0:T(8,128)(2,1)} %broadcast_multiply_fusion) | copy-start | bytes 3145732
  277.3 51.9 %copy-start.1 = (bf16[64,64,64]{2,1,0:T(8,128)(2,1)S(1)}, bf16[64,64,64]{2,1,0:T(8,128)(2,1)}, u32[]{:S(2)}) copy-start(bf16[64,64,64]{2,1,0:T(8,128)(2,1)} %param.8) | copy-start | bytes 1572868
Sparse Core Ops, SparseCore 0:
  10.0 120.0 all-gather.1
  295.1 32.7 reduce-scatter.1
